TPU v7x, 128 devices: a whole 4x4x4 slice. The times are simulated.
128 devices in a mesh: blk: 16 (over x_hi, z, core), uly: 8 (over x_lo, y).
Axes of the slice: x: 4 (x_hi: 2, x_lo: 2; x = x_hi * 2 + x_lo), y: 4, z: 4, core: 2. Of those that a mesh axis runs over, the one named last changes fastest.
Arguments:
- queries: bfloat16 [32768, 4096], P(('blk', 'uly')), may hold values from -140 to 140
- keys: bfloat16 [32768, 1024], P(('blk', 'uly')), may hold values from -6 to 6
- values: bfloat16 [32768, 1024], P(('blk', 'uly')), may hold values from -6 to 6
- doc_lengths: int32 [4], replicated, may hold values from 1 to 24576, 32768 in all
- selected: int32 [32, 8], replicated, may hold values from 0 to 30, as said below
Outputs:
- attended: bfloat16 [32768, 4096], P(('blk', 'uly'))
Inputs may be any that keep to these rules, and one draw needn't show every extreme that they name: selected[b, g] <= b, and equals b only for b = 0. For every device index along blk (blocks b with equal b // 2) and every key head, the blocks it selects that lie outside its own 2 blocks lie in distinct blocks of blk, so one other index of blk supplies at most one selected block a key head to it.
All inputs are finite; a program needn't handle non-finite values.
Results may differ from a plain program's by a relative error of at most 0.004.
Values may be sent and summed in bfloat16 or wider, within the bound.
A program may use at most 128 MiB of HBM per device.

v0:
```python
import jax
import jax.numpy as jnp
from jax import lax
from jax.sharding import PartitionSpec as P

HQ = 32
KVH = 8
HD = 128
MB = 1024


def shortened(shard):

    def short(part):
        return part.astype(jnp.bfloat16) if part.dtype == jnp.float32 else part

    return jax.tree.map(short, shard)


def on_device(queries, keys, values, doc_lengths, selected):
    q_heads, k_heads, v_heads = (
        lax.all_to_all(queries, "uly", split_axis=1, concat_axis=0, tiled=True),
        lax.all_to_all(keys, "uly", split_axis=1, concat_axis=0, tiled=True),
        lax.all_to_all(values, "uly", split_axis=1, concat_axis=0, tiled=True),
    )
    shard = k_heads.shape[0]
    kv_dev = k_heads.shape[1] // HD
    per_dev = shard // MB
    group = HQ // KVH
    scale = 1.0 / HD**0.5
    blk_index = lax.axis_index("blk")
    uly_index = lax.axis_index("uly")
    ends = jnp.cumsum(doc_lengths)

    def doc_of(places):
        return jnp.sum((ends <= places[..., None]).astype(jnp.int32), axis=-1)

    column = lax.dynamic_slice_in_dim(selected, uly_index * kv_dev, kv_dev, 1)
    mine = lax.dynamic_slice_in_dim(column, blk_index * per_dev, per_dev, 0)
    offsets = jnp.arange(MB, dtype=jnp.int32)
    k_blocks = k_heads.reshape(per_dev, MB, kv_dev, HD)
    v_blocks = v_heads.reshape(per_dev, MB, kv_dev, HD)
    empty = jnp.zeros((per_dev, kv_dev, MB, HD), jnp.bfloat16)
    k_piece = lax.all_gather(k_heads, "blk", axis=0, tiled=True)
    v_piece = lax.all_gather(v_heads, "blk", axis=0, tiled=True)
    count = k_piece.shape[0]
    wanted_rows = mine[:, :, None] * MB + offsets
    inside = (wanted_rows >= 0) & (wanted_rows < count)
    index = jnp.clip(wanted_rows, 0, count - 1)
    head_rows = jnp.arange(kv_dev, dtype=jnp.int32)[None, :, None]
    k_got = k_piece.reshape(count, kv_dev, HD)[index, head_rows]
    v_got = v_piece.reshape(count, kv_dev, HD)[index, head_rows]
    chosen_k = jnp.where(inside[..., None], k_got, empty)
    chosen_v = jnp.where(inside[..., None], v_got, empty)
    doc_query = doc_of(blk_index * shard + jnp.arange(shard, dtype=jnp.int32)).reshape(per_dev, MB)
    doc_chosen = doc_of(mine[:, :, None] * MB + offsets)
    live = mine != (blk_index * per_dev + jnp.arange(per_dev, dtype=jnp.int32))[:, None]
    q_five = q_heads.reshape(per_dev, MB, kv_dev, group, HD)
    causal = offsets[:, None] >= offsets[None, :]

    def one_block(row):
        q_now = q_five[row, :, 0]
        own_k = k_blocks[row, :, 0]
        own_v = v_blocks[row, :, 0]
        doc_now = doc_query[row]
        own_scores = (
            jnp.einsum("mgd,nd->gmn", q_now, own_k, preferred_element_type=jnp.float32) * scale
        )
        sel_scores = (
            jnp.einsum("mgd,nd->gmn", q_now, chosen_k[row, 0], preferred_element_type=jnp.float32)
            * scale
        )
        own_mask = causal & (doc_now[:, None] == doc_now[None, :])
        sel_mask = (doc_now[:, None] == doc_chosen[row, 0][None, :]) & live[row, 0]
        top = jnp.maximum(
            jnp.max(jnp.where(own_mask, own_scores, -jnp.inf), axis=-1),
            jnp.max(jnp.where(sel_mask, sel_scores, -jnp.inf), axis=-1),
        )
        own_weight = jnp.where(own_mask, jnp.exp(own_scores - top[..., None]), 0.0)
        sel_weight = jnp.where(sel_mask, jnp.exp(sel_scores - top[..., None]), 0.0)
        total = jnp.sum(own_weight, axis=-1) + jnp.sum(sel_weight, axis=-1)
        acc = jnp.einsum(
            "gmn,nd->mgd",
            own_weight.astype(jnp.bfloat16),
            own_v,
            preferred_element_type=jnp.float32,
        )
        acc = acc + jnp.einsum(
            "gmn,nd->mgd",
            sel_weight.astype(jnp.bfloat16),
            chosen_v[row, 0],
            preferred_element_type=jnp.float32,
        )
        output = (acc / jnp.transpose(total)[:, :, None]).astype(jnp.bfloat16)
        results = [output.reshape(MB, group * HD)]
        return jnp.concatenate(results, axis=1)

    blocks = lax.map(one_block, jnp.arange(per_dev, dtype=jnp.int32))
    head_major = blocks.reshape(shard, kv_dev * group * HD)
    return lax.all_to_all(
        shortened(head_major), "uly", split_axis=0, concat_axis=1, tiled=True
    ).astype(head_major.dtype)


def solution(mesh):
    placed = (P(("blk", "uly"), None), P(("blk", "uly"), None), P(("blk", "uly"), None), P(), P())
    return jax.shard_map(
        on_device, mesh=mesh, in_specs=placed, out_specs=P(("blk", "uly"), None), check_vma=False
    )
```

profile of v0, /device:TPU:0, one launch (start us, length us, event | category | flops | bytes accessed | tf_op | source)
XLA Modules:
  0.0 339.3 jit_solution(10035589432104716026)
XLA Ops:
  6.5 0.0 copy-start
  6.5 0.0 all-gather.5.cloned.1.call-start
  6.5 1.3 copy.43
  7.8 15.3 %all_to_all.73 = bf16[256,8,128]{0,2,1:T(8,128)(2,1)S(1)} all-to-all(bf16[256,8,128]{0,2,1:T(8,128)(2,1)S(1)} %bitcast.166), channel_id=1, replica_groups=mesh['blk'=16,'uly'=8] {'uly'}, dimensions={1} | all-to-all | bytes 1048576 | tf_op jit(solution)/shard_map/all_to_all | solution.py:24
  23.2 1.0 copy.44
  24.2 0.0 copy-start.2
  24.2 0.0 all-gather.5.cloned.1.call-update
  24.2 0.0 all-gather.3.cloned.1.call-start
  24.3 0.0 copy-done
  24.3 0.1 copy_bitcast_fusion.4
  24.4 11.7 %all_to_all.74 = bf16[256,8,128]{2,0,1:T(8,128)(2,1)} all-to-all(bf16[256,8,128]{2,0,1:T(8,128)(2,1)S(1)} %copy_bitcast_fusion.4), channel_id=1, replica_groups=mesh['blk'=16,'uly'=8] {'uly'}, dimensions={1} | all-to-all | bytes 1048576 | tf_op jit(solution)/shard_map/all_to_all | solution.py:23
  36.1 0.0 all-gather.3.cloned.1.call-update
  36.1 3.1 copy.80
  39.3 3.6 %all-to-all-start.2 = ((bf16[256,8,512]{2,0,1:T(8,128)(2,1)}), bf16[256,8,512]{2,0,1:T(8,128)(2,1)S(1)}, u32[]{:S(2)}, u32[]{:S(2)}) async-start(bf16[256,8,512]{2,0,1:T(8,128)(2,1)} %bitcast.154), calls=%async_computation.2 | async-start | bytes 4194304 | tf_op jit(solution)/shard_map/all_to_all | solution.py:22
  42.9 0.8 dynamic_slice.32
  43.7 0.1 copy.66
  43.8 0.1 multiply_reduce_fusion
  43.9 0.1 compare_select_fusion
  44.0 0.8 reduce-window.8
  44.9 0.1 convert_reduce_fusion.1
  45.0 0.1 iota_add_fusion
  45.0 0.1 convert_reduce_fusion
  45.2 0.1 compare_and_fusion.1
  45.2 27.4 %all-to-all-done.2 = bf16[256,8,512]{2,0,1:T(8,128)(2,1)S(1)} async-done(((bf16[256,8,512]{2,0,1:T(8,128)(2,1)}), bf16[256,8,512]{2,0,1:T(8,128)(2,1)S(1)}, u32[]{:S(2)}, u32[]{:S(2)}) %all-to-all-start.2) | async-done | bytes 2097184 | tf_op jit(solution)/shard_map/all_to_all | solution.py:22
  72.6 2.1 reshape.225
  74.7 27.1 %all-gather.5.cloned.1.call-done = bf16[32768,128]{1,0:T(8,128)(2,1)} async-done(((bf16[2048,128]{1,0:T(8,128)(2,1)}), bf16[32768,128]{1,0:T(8,128)(2,1)}) %all-gather.5.cloned.1.call-update) | async-done | bytes 8388624 | tf_op jit(solution)/shard_map/all_gather | solution.py:45
  101.8 22.6 %gather_fusion.1 = bf16[2048,128]{1,0:T(8,128)(2,1)S(1)} fusion(bf16[32768,1,128]{2,0,1:T(8,128)(2,1)} %bitcast.157, s32[2048]{0:T(1024)S(1)} %bitcast.150), kind=kCustom, calls=%fused_computation.1 | custom fusion | bytes 1064960 | tf_op jit(solution)/shard_map/gather | solution.py:52
  124.4 0.2 copy.50
  124.7 50.9 %all-gather.3.cloned.1.call-done = bf16[32768,128]{1,0:T(8,128)(2,1)} async-done(((bf16[2048,128]{1,0:T(8,128)(2,1)}), bf16[32768,128]{1,0:T(8,128)(2,1)}) %all-gather.3.cloned.1.call-update) | async-done | bytes 8388624 | tf_op jit(solution)/shard_map/all_gather | solution.py:44
  175.6 22.6 %gather_fusion = bf16[2048,128]{1,0:T(8,128)(2,1)S(1)} fusion(bf16[32768,1,128]{2,0,1:T(8,128)(2,1)} %bitcast.158, s32[2048]{0:T(1024)S(1)} %bitcast.151), kind=kCustom, calls=%fused_computation | custom fusion | bytes 1064960 | tf_op jit(solution)/shard_map/gather | solution.py:51
  198.2 0.2 copy.48
  198.4 1.1 broadcast_select_fusion
  199.5 0.0 copy-done.2
  199.5 94.8 %while.11 = (s32[]{:T(128)}, bf16[2,1024,512]{2,1,0:T(8,128)(2,1)}, s32[2]{0:T(128)S(1)}, bf16[2,1024,1,128]{3,1,0,2:T(8,128)(2,1)S(1)}, s32[2,1024]{1,0:T(2,128...) while((s32[]{:T(128)}, bf16[2,1024,512]{2,1,0:T(8,128)(2,1)}, ...), condition=%wide.region_8.9_spmd.clone, body=%wide.region_3.8_spmd.clone.sunk | while | flops 4394049536 | bytes 123986648 | solution.py:98
  199.5 0.6 dynamic_slice.83
  202.0 0.6 constant_dynamic-slice_fusion.10
  202.5 2.5 compare_and_fusion.3
  205.0 1.6 constant_dynamic-slice_fusion.11
  206.6 4.0 %fusion.59 = (f32[4,1024]{1,0:T(4,128)S(1)}, f32[1024,1024,4]{1,0,2:T(8,128)S(1)}) fusion(pred[1024,1024]{0,1:T(8,128)(4,1)S(1)} %get-tuple-element.245, bf16[1,1024,1,4,128]{4,3,1,0,2:T(4,128)(2,1)S(1)} %constant_dynamic-slice_fusion.11, bf16[2,1024,1,128]{3,1,2,0:T(8,128)(2,1)} %get-tuple-element.284, s32[]{:T(128)S(6)} %select_n.115), kind=kOutput, calls=%fused_computation.10.clone.1 | convolution fusion | flops 1086320640 | bytes 19152900 | tf_op jit(solution)/shard_map/while/body/eval_jaxpr/mgd,nd->gmn/dot_general | solution.py:67
  210.6 8.5 %fusion.58 = (f32[4,1024]{1,0:T(4,128)S(1)}, f32[1024,1024,4]{1,0,2:T(8,128)}) fusion(pred[1024,1024]{0,1:T(8,128)(4,1)S(1)} %get-tuple-element.243, bf16[1,1024,1,4,128]{4,3,1,0,2:T(4,128)(2,1)S(1)} %constant_dynamic-slice_fusion.11, bf16[2,1,1024,128]{2,3,1,0:T(8,128)(2,1)} %get-tuple-element.288, s32[]{:T(128)S(6)} %select_n.115), kind=kOutput, calls=%fused_computation.5.clone.1 | convolution fusion | flops 1086320640 | bytes 19152900 | tf_op jit(solution)/shard_map/while/body/eval_jaxpr/mgd,nd->gmn/dot_general | solution.py:70
  219.1 9.9 %fusion.61 = (f32[4,1024]{1,0:T(4,128)S(1)}, f32[4,1024]{1,0:T(4,128)S(1)}) fusion(f32[1024,1024,4]{1,0,2:T(8,128)} %get-tuple-element.244, f32[4,1024]{1,0:T(4,128)S(1)} %max.13, pred[1024,1024]{0,1:T(8,128)(4,1)S(1)} %get-tuple-element.243, f32[1024,1024,4]{1,0,2:T(8,128)S(1)} %get-tuple-element.248, pred[1024,1024]{0,1:T(8,128)(4,1)S(1)} %get-tuple-element.245), kind=kLoop, calls=%fused_computation.15.clone.1 | loop fusion | flops 33546240 | bytes 35700736 | tf_op jit(solution)/shard_map/while/body/eval_jaxpr/reduce_sum | solution.py:81
  229.1 11.0 %fusion.60 = f32[128,4,1024]{2,0,1:T(8,128)} fusion(f32[1024,1024,4]{1,0,2:T(8,128)} %get-tuple-element.244, f32[4,1024]{1,0:T(4,128)S(1)} %max.13, pred[1024,1024]{0,1:T(8,128)(4,1)S(1)} %get-tuple-element.243, bf16[2,1,1024,128]{2,3,1,0:T(8,128)(2,1)} %get-tuple-element.289, s32[]{:T(128)S(6)} %select_n.115), kind=kOutput, calls=%fused_computation.17.clone.1 | convolution fusion | flops 1090519040 | bytes 20201476 | tf_op jit(solution)/shard_map/while/body/eval_jaxpr/gmn,nd->mgd/dot_general | solution.py:88
  240.1 5.2 %fusion.62 = bf16[1024,4,128]{0,2,1:T(8,128)(2,1)S(1)} fusion(f32[128,4,1024]{2,0,1:T(8,128)} %fusion.60, f32[1024,1024,4]{1,0,2:T(8,128)S(1)} %get-tuple-element.248, f32[4,1024]{1,0:T(4,128)S(1)} %max.13, pred[1024,1024]{0,1:T(8,128)(4,1)S(1)} %get-tuple-element.245, f32[1024,4]{0,1:T(4,128)S(1)} %add_bitcast_fusion.2, ...), kind=kOutput, calls=%fused_computation.25.clone.1 | convolution fusion | flops 1092091904 | bytes 21266436 | tf_op jit(solution)/shard_map/while/body/eval_jaxpr/gmn,nd->mgd/dot_general | solution.py:82
  245.3 0.5 copy.87
  245.9 1.0 constant_dynamic-update-slice_fusion.2
  246.9 0.6 dynamic_slice.83
  249.4 0.6 constant_dynamic-slice_fusion.10
  249.9 2.5 compare_and_fusion.3
  252.4 1.6 constant_dynamic-slice_fusion.11
  254.0 4.0 %fusion.59 = (f32[4,1024]{1,0:T(4,128)S(1)}, f32[1024,1024,4]{1,0,2:T(8,128)S(1)}) fusion(pred[1024,1024]{0,1:T(8,128)(4,1)S(1)} %get-tuple-element.245, bf16[1,1024,1,4,128]{4,3,1,0,2:T(4,128)(2,1)S(1)} %constant_dynamic-slice_fusion.11, bf16[2,1024,1,128]{3,1,2,0:T(8,128)(2,1)} %get-tuple-element.284, s32[]{:T(128)S(6)} %select_n.115), kind=kOutput, calls=%fused_computation.10.clone.1 | convolution fusion | flops 1086320640 | bytes 19152900 | tf_op jit(solution)/shard_map/while/body/eval_jaxpr/mgd,nd->gmn/dot_general | solution.py:67
  258.0 8.5 %fusion.58 = (f32[4,1024]{1,0:T(4,128)S(1)}, f32[1024,1024,4]{1,0,2:T(8,128)}) fusion(pred[1024,1024]{0,1:T(8,128)(4,1)S(1)} %get-tuple-element.243, bf16[1,1024,1,4,128]{4,3,1,0,2:T(4,128)(2,1)S(1)} %constant_dynamic-slice_fusion.11, bf16[2,1,1024,128]{2,3,1,0:T(8,128)(2,1)} %get-tuple-element.288, s32[]{:T(128)S(6)} %select_n.115), kind=kOutput, calls=%fused_computation.5.clone.1 | convolution fusion | flops 1086320640 | bytes 19152900 | tf_op jit(solution)/shard_map/while/body/eval_jaxpr/mgd,nd->gmn/dot_general | solution.py:70
  266.5 9.9 %fusion.61 = (f32[4,1024]{1,0:T(4,128)S(1)}, f32[4,1024]{1,0:T(4,128)S(1)}) fusion(f32[1024,1024,4]{1,0,2:T(8,128)} %get-tuple-element.244, f32[4,1024]{1,0:T(4,128)S(1)} %max.13, pred[1024,1024]{0,1:T(8,128)(4,1)S(1)} %get-tuple-element.243, f32[1024,1024,4]{1,0,2:T(8,128)S(1)} %get-tuple-element.248, pred[1024,1024]{0,1:T(8,128)(4,1)S(1)} %get-tuple-element.245), kind=kLoop, calls=%fused_computation.15.clone.1 | loop fusion | flops 33546240 | bytes 35700736 | tf_op jit(solution)/shard_map/while/body/eval_jaxpr/reduce_sum | solution.py:81
  276.5 11.0 %fusion.60 = f32[128,4,1024]{2,0,1:T(8,128)} fusion(f32[1024,1024,4]{1,0,2:T(8,128)} %get-tuple-element.244, f32[4,1024]{1,0:T(4,128)S(1)} %max.13, pred[1024,1024]{0,1:T(8,128)(4,1)S(1)} %get-tuple-element.243, bf16[2,1,1024,128]{2,3,1,0:T(8,128)(2,1)} %get-tuple-element.289, s32[]{:T(128)S(6)} %select_n.115), kind=kOutput, calls=%fused_computation.17.clone.1 | convolution fusion | flops 1090519040 | bytes 20201476 | tf_op jit(solution)/shard_map/while/body/eval_jaxpr/gmn,nd->mgd/dot_general | solution.py:88
  287.4 5.2 %fusion.62 = bf16[1024,4,128]{0,2,1:T(8,128)(2,1)S(1)} fusion(f32[128,4,1024]{2,0,1:T(8,128)} %fusion.60, f32[1024,1024,4]{1,0,2:T(8,128)S(1)} %get-tuple-element.248, f32[4,1024]{1,0:T(4,128)S(1)} %max.13, pred[1024,1024]{0,1:T(8,128)(4,1)S(1)} %get-tuple-element.245, f32[1024,4]{0,1:T(4,128)S(1)} %add_bitcast_fusion.2, ...), kind=kOutput, calls=%fused_computation.25.clone.1 | convolution fusion | flops 1092091904 | bytes 21266436 | tf_op jit(solution)/shard_map/while/body/eval_jaxpr/gmn,nd->mgd/dot_general | solution.py:82
  292.7 0.5 copy.87
  293.2 1.0 constant_dynamic-update-slice_fusion.2
  294.3 0.0 copy-start.1
  294.3 31.7 %all_to_all.75 = bf16[8,256,512]{2,1,0:T(8,128)(2,1)S(1)} all-to-all(bf16[8,256,512]{2,1,0:T(8,128)(2,1)} %bitcast.160), channel_id=1, replica_groups=mesh['blk'=16,'uly'=8] {'uly'}, dimensions={0} | all-to-all | bytes 4194304 | tf_op jit(solution)/shard_map/all_to_all | solution.py:100
  326.0 2.4 copy.56
  328.4 4.1 %copy.57 = bf16[256,4096]{1,0:T(8,128)(2,1)} copy(bf16[256,4096]{0,1:T(8,128)(2,1)} %bitcast.156) | data formatting | bytes 4194304 | tf_op jit(solution)/shard_map/all_to_all | solution.py:100
  332.4 0.0 copy-done.1
  (16 shorter events, 0.1 us)
Async XLA Ops:
  6.5 17.7 %copy-start = (bf16[256,1024]{1,0:T(8,128)(2,1)S(1)}, bf16[256,1024]{1,0:T(8,128)(2,1)}, u32[]{:S(2)}) copy-start(bf16[256,1024]{1,0:T(8,128)(2,1)} %param.8) | copy-start | bytes 1572868
  6.5 95.3 %all-gather.5.cloned.1.call-start = ((), (), s32[]{:S(2)}) async-start(), calls=%async_computation.5 | async-start | bytes 8912896 | tf_op jit(solution)/shard_map/all_gather | solution.py:45
  24.2 175.3 %copy-start.2 = (bf16[8,256,128]{2,1,0:T(8,128)(2,1)S(1)}, bf16[8,256,128]{2,1,0:T(8,128)(2,1)}, u32[]{:S(2)}) copy-start(bf16[8,256,128]{2,1,0:T(8,128)(2,1)} %copy.44) | copy-start | bytes 1572868
  24.2 151.4 %all-gather.3.cloned.1.call-start = ((), (), s32[]{:S(2)}) async-start(), calls=%async_computation.4 | async-start | bytes 8912896 | tf_op jit(solution)/shard_map/all_gather | solution.py:44
  39.3 33.4 %all-to-all-start.2 = ((bf16[256,8,512]{2,0,1:T(8,128)(2,1)}), bf16[256,8,512]{2,0,1:T(8,128)(2,1)S(1)}, u32[]{:S(2)}, u32[]{:S(2)}) async-start(bf16[256,8,512]{2,0,1:T(8,128)(2,1)} %bitcast.154), calls=%async_computation.2 | async-start | bytes 4194304 | tf_op jit(solution)/shard_map/all_to_all | solution.py:22
  294.3 38.1 %copy-start.1 = (bf16[256,1024]{1,0:T(8,128)(2,1)S(1)}, bf16[256,1024]{1,0:T(8,128)(2,1)}, u32[]{:S(2)}) copy-start(bf16[256,1024]{1,0:T(8,128)(2,1)} %param.8) | copy-start | bytes 1572868
Sparse Core Ops, SparseCore 0:
  24.3 77.4 all-gather.4
  104.3 71.2 all-gather.2
where the time goes:
time: 341 us; the launch traced here: 339 us
  waiting for transfers between devices  105 us (31%)
  local copies, waits for them, and re-layouts  69.3 us (20%)
  blocking collectives  58.8 us (17%)
  matrix products  57.4 us (17%)
  other arithmetic  27.3 us (8%)
  between operations  13.5 us (4%)
  loops' own time  3.8 us (1%)
  starting transfers between devices  3.65 us (1%)
    all_gather x1, waiting for transfers between devices, on_device(): k_piece = lax.all_gather(k_heads, 'blk', axis=0, tiled=True)  50.9 us
    all_to_all x1, blocking collectives, on_device(): lax.all_to_all(shortened(head_major), 'uly', split_axis=0, concat_axis=1,...  31.7 us
    all_to_all x1, waiting for transfers between devices, on_device(): lax.all_to_all(queries, 'uly', split_axis=1, concat_axis=0, tiled=True)  27.4 us
    all_gather x1, waiting for transfers between devices, on_device(): v_piece = lax.all_gather(v_heads, 'blk', axis=0, tiled=True)  27.1 us
    gather x2, local copies, waits for them, and re-layouts, on_device(): v_got = v_piece.reshape(count, kv_dev, HD)[index, head_rows]  22.8 us
    gather x2, local copies, waits for them, and re-layouts, on_device(): k_got = k_piece.reshape(count, kv_dev, HD)[index, head_rows]  22.8 us
    dot_general x2, matrix products, one_block(): jnp.einsum('gmn,nd->mgd', sel_weight.astype(jnp.bfloat16), chosen_v[row,...  21.9 us
    reduce_sum x2, other arithmetic, one_block(): total = jnp.sum(own_weight, axis=-1) + jnp.sum(sel_weight, axis=-1)  19.9 us
  transfers between devices with their start and end apart: 3, of which 3 were waited for; matrix products, arithmetic and copies ran while one was open for 9% of the time, Pallas kernels for 0%

commit v1 on v0

--- a/solution.py
+++ b/solution.py
@@ -19,7 +19,12 @@
 
 def on_device(queries, keys, values, doc_lengths, selected):
     q_heads, k_heads, v_heads = (
-        lax.all_to_all(queries, "uly", split_axis=1, concat_axis=0, tiled=True),
+        jnp.concatenate(
+            lax.all_to_all(
+                jnp.stack(jnp.split(queries, lax.axis_size("uly"), axis=1)), "uly", 0, 0
+            ),
+            axis=0,
+        ),
         lax.all_to_all(keys, "uly", split_axis=1, concat_axis=0, tiled=True),
         lax.all_to_all(values, "uly", split_axis=1, concat_axis=0, tiled=True),
     )

time: 341 us -> 344 us (level)
  local copies, waits for them, and re-layouts: 69.3 us -> 72.9 us
    unnamed x9 -> x20, local copies, waits for them, and re-layouts: 1.41 us -> 7.41 us
where the time goes in v1:
time: 344 us; the launch traced here: 343 us
  waiting for transfers between devices  106 us (31%)
  local copies, waits for them, and re-layouts  72.9 us (21%)
  blocking collectives  58.8 us (17%)
  matrix products  57.4 us (17%)
  other arithmetic  26.7 us (8%)
  between operations  13.6 us (4%)
  loops' own time  3.8 us (1%)
  starting transfers between devices  3.65 us (1%)
    all_gather x1, waiting for transfers between devices, on_device(): k_piece = lax.all_gather(k_heads, 'blk', axis=0, tiled=True)  51 us
    all_to_all x1, blocking collectives, on_device(): lax.all_to_all(shortened(head_major), 'uly', split_axis=0, concat_axis=1,...  31.5 us
    all_to_all x1, waiting for transfers between devices, on_device(): lax.all_to_all(jnp.stack(jnp.split(queries, lax.axis_size('uly'), axis=1)...  30.7 us
    all_gather x1, waiting for transfers between devices, on_device(): v_piece = lax.all_gather(v_heads, 'blk', axis=0, tiled=True)  24.3 us
    gather x2, local copies, waits for them, and re-layouts, on_device(): v_got = v_piece.reshape(count, kv_dev, HD)[index, head_rows]  22.8 us
    gather x2, local copies, waits for them, and re-layouts, on_device(): k_got = k_piece.reshape(count, kv_dev, HD)[index, head_rows]  22.8 us
    dot_general x2, matrix products, one_block(): jnp.einsum('gmn,nd->mgd', sel_weight.astype(jnp.bfloat16), chosen_v[row,...  21.9 us
    reduce_sum x2, other arithmetic, one_block(): total = jnp.sum(own_weight, axis=-1) + jnp.sum(sel_weight, axis=-1)  19.9 us
  transfers between devices with their start and end apart: 3, of which 3 were waited for; matrix products, arithmetic and copies ran while one was open for 9% of the time, Pallas kernels for 0%

profile of v1, /device:TPU:0, one launch (start us, length us, event | category | flops | bytes accessed | tf_op | source)
XLA Modules:
  0.0 342.8 jit_solution(9090520632633852566)
XLA Ops:
  6.5 0.0 all-gather.5.cloned.1.call-start
  6.5 2.2 copy.41
  8.7 15.5 %all_to_all.62 = bf16[256,8,128]{0,2,1:T(8,128)(2,1)S(1)} all-to-all(bf16[256,8,128]{0,2,1:T(8,128)(2,1)} %bitcast.172), channel_id=1, replica_groups=mesh['blk'=16,'uly'=8] {'uly'}, dimensions={1} | all-to-all | bytes 1048576 | tf_op jit(solution)/shard_map/all_to_all | solution.py:29
  24.3 1.0 copy.42
  25.3 0.0 all-gather.5.cloned.1.call-update
  25.3 0.0 all-gather.3.cloned.1.call-start
  25.3 0.0 copy-done
  25.4 0.1 copy_bitcast_fusion.3
  25.5 11.7 %all_to_all.63 = bf16[256,8,128]{2,0,1:T(8,128)(2,1)} all-to-all(bf16[256,8,128]{2,0,1:T(8,128)(2,1)S(1)} %copy_bitcast_fusion.3), channel_id=1, replica_groups=mesh['blk'=16,'uly'=8] {'uly'}, dimensions={1} | all-to-all | bytes 1048576 | tf_op jit(solution)/shard_map/all_to_all | solution.py:28
  37.2 0.0 all-gather.3.cloned.1.call-update
  37.2 0.0 copy-start.4
  37.2 0.7 bitcast_dynamic-update-slice_fusion.7
  37.9 0.7 bitcast_dynamic-update-slice_fusion.6
  38.7 0.7 bitcast_dynamic-update-slice_fusion.5
  39.4 0.7 bitcast_dynamic-update-slice_fusion.4
  40.1 0.7 bitcast_dynamic-update-slice_fusion.3
  40.9 0.7 bitcast_dynamic-update-slice_fusion.2
  41.6 0.7 bitcast_dynamic-update-slice_fusion.1
  42.3 0.7 bitcast_dynamic-update-slice_fusion
  43.1 3.6 %all-to-all-start.2 = ((bf16[8,256,512]{2,1,0:T(8,128)(2,1)}), bf16[8,256,512]{2,1,0:T(8,128)(2,1)S(1)}, u32[]{:S(2)}, u32[]{:S(2)}) async-start(bf16[8,256,512]{2,1,0:T(8,128)(2,1)} %bitcast_dynamic-update-slice_fusion), calls=%async_computation.2 | async-start | bytes 4194304 | tf_op jit(solution)/shard_map/all_to_all | solution.py:23
  46.7 0.8 dynamic_slice.32
  47.5 0.1 copy.63
  47.6 0.1 multiply_reduce_fusion
  47.7 0.1 compare_select_fusion
  47.8 0.2 reduce-window.8
  48.0 0.1 convert_reduce_fusion.1
  48.1 0.1 iota_add_fusion
  48.2 0.1 convert_reduce_fusion
  48.3 0.1 compare_and_fusion.1
  48.4 30.7 %all-to-all-done.2 = bf16[8,256,512]{2,1,0:T(8,128)(2,1)S(1)} async-done(((bf16[8,256,512]{2,1,0:T(8,128)(2,1)}), bf16[8,256,512]{2,1,0:T(8,128)(2,1)S(1)}, u32[]{:S(2)}, u32[]{:S(2)}) %all-to-all-start.2) | async-done | bytes 2097184 | tf_op jit(solution)/shard_map/all_to_all | solution.py:23
  79.1 2.1 reshape_reshape.3
  81.1 24.3 %all-gather.5.cloned.1.call-done = bf16[32768,128]{1,0:T(8,128)(2,1)} async-done(((bf16[2048,128]{1,0:T(8,128)(2,1)}), bf16[32768,128]{1,0:T(8,128)(2,1)}) %all-gather.5.cloned.1.call-update) | async-done | bytes 8388624 | tf_op jit(solution)/shard_map/all_gather | solution.py:50
  105.4 22.6 %gather_fusion.1 = bf16[2048,128]{1,0:T(8,128)(2,1)S(1)} fusion(bf16[32768,1,128]{2,0,1:T(8,128)(2,1)} %bitcast.166, s32[2048]{0:T(1024)S(1)} %bitcast.161), kind=kCustom, calls=%fused_computation.1 | custom fusion | bytes 1064960 | tf_op jit(solution)/shard_map/gather | solution.py:57
  128.1 0.2 copy.47
  128.3 51.0 %all-gather.3.cloned.1.call-done = bf16[32768,128]{1,0:T(8,128)(2,1)} async-done(((bf16[2048,128]{1,0:T(8,128)(2,1)}), bf16[32768,128]{1,0:T(8,128)(2,1)}) %all-gather.3.cloned.1.call-update) | async-done | bytes 8388624 | tf_op jit(solution)/shard_map/all_gather | solution.py:49
  179.3 22.6 %gather_fusion = bf16[2048,128]{1,0:T(8,128)(2,1)S(1)} fusion(bf16[32768,1,128]{2,0,1:T(8,128)(2,1)} %bitcast.167, s32[2048]{0:T(1024)S(1)} %bitcast.162), kind=kCustom, calls=%fused_computation | custom fusion | bytes 1064960 | tf_op jit(solution)/shard_map/gather | solution.py:56
  201.9 0.2 copy.45
  202.1 1.1 broadcast_select_fusion
  203.2 94.8 %while.11 = (s32[]{:T(128)}, bf16[2,1024,512]{2,1,0:T(8,128)(2,1)}, s32[2]{0:T(128)S(1)}, bf16[2,1024,1,128]{3,1,0,2:T(8,128)(2,1)S(1)}, s32[2,1024]{1,0:T(2,128...) while((s32[]{:T(128)}, bf16[2,1024,512]{2,1,0:T(8,128)(2,1)}, ...), condition=%wide.region_8.9_spmd.clone, body=%wide.region_3.8_spmd.clone.sunk | while | flops 4394049536 | bytes 123986648 | solution.py:103
  203.2 0.6 dynamic_slice.83
  205.7 0.6 constant_dynamic-slice_fusion.10
  206.2 2.5 compare_and_fusion.3
  208.7 1.6 constant_dynamic-slice_fusion.11
  210.3 4.0 %fusion.59 = (f32[4,1024]{1,0:T(4,128)S(1)}, f32[1024,1024,4]{1,0,2:T(8,128)S(1)}) fusion(pred[1024,1024]{0,1:T(8,128)(4,1)S(1)} %get-tuple-element.245, bf16[1,1024,1,4,128]{4,3,1,0,2:T(4,128)(2,1)S(1)} %constant_dynamic-slice_fusion.11, bf16[2,1024,1,128]{3,1,2,0:T(8,128)(2,1)} %get-tuple-element.284, s32[]{:T(128)S(6)} %select_n.115), kind=kOutput, calls=%fused_computation.10.clone.1 | convolution fusion | flops 1086320640 | bytes 19152900 | tf_op jit(solution)/shard_map/while/body/eval_jaxpr/mgd,nd->gmn/dot_general | solution.py:72
  214.3 8.5 %fusion.58 = (f32[4,1024]{1,0:T(4,128)S(1)}, f32[1024,1024,4]{1,0,2:T(8,128)}) fusion(pred[1024,1024]{0,1:T(8,128)(4,1)S(1)} %get-tuple-element.243, bf16[1,1024,1,4,128]{4,3,1,0,2:T(4,128)(2,1)S(1)} %constant_dynamic-slice_fusion.11, bf16[2,1,1024,128]{2,3,1,0:T(8,128)(2,1)} %get-tuple-element.288, s32[]{:T(128)S(6)} %select_n.115), kind=kOutput, calls=%fused_computation.5.clone.1 | convolution fusion | flops 1086320640 | bytes 19152900 | tf_op jit(solution)/shard_map/while/body/eval_jaxpr/mgd,nd->gmn/dot_general | solution.py:75
  222.8 9.9 %fusion.61 = (f32[4,1024]{1,0:T(4,128)S(1)}, f32[4,1024]{1,0:T(4,128)S(1)}) fusion(f32[1024,1024,4]{1,0,2:T(8,128)} %get-tuple-element.244, f32[4,1024]{1,0:T(4,128)S(1)} %max.13, pred[1024,1024]{0,1:T(8,128)(4,1)S(1)} %get-tuple-element.243, f32[1024,1024,4]{1,0,2:T(8,128)S(1)} %get-tuple-element.248, pred[1024,1024]{0,1:T(8,128)(4,1)S(1)} %get-tuple-element.245), kind=kLoop, calls=%fused_computation.15.clone.1 | loop fusion | flops 33546240 | bytes 35700736 | tf_op jit(solution)/shard_map/while/body/eval_jaxpr/reduce_sum | solution.py:86
  232.8 11.0 %fusion.60 = f32[128,4,1024]{2,0,1:T(8,128)} fusion(f32[1024,1024,4]{1,0,2:T(8,128)} %get-tuple-element.244, f32[4,1024]{1,0:T(4,128)S(1)} %max.13, pred[1024,1024]{0,1:T(8,128)(4,1)S(1)} %get-tuple-element.243, bf16[2,1,1024,128]{2,3,1,0:T(8,128)(2,1)} %get-tuple-element.289, s32[]{:T(128)S(6)} %select_n.115), kind=kOutput, calls=%fused_computation.17.clone.1 | convolution fusion | flops 1090519040 | bytes 20201476 | tf_op jit(solution)/shard_map/while/body/eval_jaxpr/gmn,nd->mgd/dot_general | solution.py:93
  243.7 5.2 %fusion.62 = bf16[1024,4,128]{0,2,1:T(8,128)(2,1)S(1)} fusion(f32[128,4,1024]{2,0,1:T(8,128)} %fusion.60, f32[1024,1024,4]{1,0,2:T(8,128)S(1)} %get-tuple-element.248, f32[4,1024]{1,0:T(4,128)S(1)} %max.13, pred[1024,1024]{0,1:T(8,128)(4,1)S(1)} %get-tuple-element.245, f32[1024,4]{0,1:T(4,128)S(1)} %add_bitcast_fusion.2, ...), kind=kOutput, calls=%fused_computation.25.clone.1 | convolution fusion | flops 1092091904 | bytes 21266436 | tf_op jit(solution)/shard_map/while/body/eval_jaxpr/gmn,nd->mgd/dot_general | solution.py:87
  249.0 0.5 copy.81
  249.6 1.0 constant_dynamic-update-slice_fusion.2
  250.6 0.6 dynamic_slice.83
  253.1 0.6 constant_dynamic-slice_fusion.10
  253.6 2.5 compare_and_fusion.3
  256.1 1.6 constant_dynamic-slice_fusion.11
  257.7 4.0 %fusion.59 = (f32[4,1024]{1,0:T(4,128)S(1)}, f32[1024,1024,4]{1,0,2:T(8,128)S(1)}) fusion(pred[1024,1024]{0,1:T(8,128)(4,1)S(1)} %get-tuple-element.245, bf16[1,1024,1,4,128]{4,3,1,0,2:T(4,128)(2,1)S(1)} %constant_dynamic-slice_fusion.11, bf16[2,1024,1,128]{3,1,2,0:T(8,128)(2,1)} %get-tuple-element.284, s32[]{:T(128)S(6)} %select_n.115), kind=kOutput, calls=%fused_computation.10.clone.1 | convolution fusion | flops 1086320640 | bytes 19152900 | tf_op jit(solution)/shard_map/while/body/eval_jaxpr/mgd,nd->gmn/dot_general | solution.py:72
  261.7 8.5 %fusion.58 = (f32[4,1024]{1,0:T(4,128)S(1)}, f32[1024,1024,4]{1,0,2:T(8,128)}) fusion(pred[1024,1024]{0,1:T(8,128)(4,1)S(1)} %get-tuple-element.243, bf16[1,1024,1,4,128]{4,3,1,0,2:T(4,128)(2,1)S(1)} %constant_dynamic-slice_fusion.11, bf16[2,1,1024,128]{2,3,1,0:T(8,128)(2,1)} %get-tuple-element.288, s32[]{:T(128)S(6)} %select_n.115), kind=kOutput, calls=%fused_computation.5.clone.1 | convolution fusion | flops 1086320640 | bytes 19152900 | tf_op jit(solution)/shard_map/while/body/eval_jaxpr/mgd,nd->gmn/dot_general | solution.py:75
  270.2 9.9 %fusion.61 = (f32[4,1024]{1,0:T(4,128)S(1)}, f32[4,1024]{1,0:T(4,128)S(1)}) fusion(f32[1024,1024,4]{1,0,2:T(8,128)} %get-tuple-element.244, f32[4,1024]{1,0:T(4,128)S(1)} %max.13, pred[1024,1024]{0,1:T(8,128)(4,1)S(1)} %get-tuple-element.243, f32[1024,1024,4]{1,0,2:T(8,128)S(1)} %get-tuple-element.248, pred[1024,1024]{0,1:T(8,128)(4,1)S(1)} %get-tuple-element.245), kind=kLoop, calls=%fused_computation.15.clone.1 | loop fusion | flops 33546240 | bytes 35700736 | tf_op jit(solution)/shard_map/while/body/eval_jaxpr/reduce_sum | solution.py:86
  280.2 11.0 %fusion.60 = f32[128,4,1024]{2,0,1:T(8,128)} fusion(f32[1024,1024,4]{1,0,2:T(8,128)} %get-tuple-element.244, f32[4,1024]{1,0:T(4,128)S(1)} %max.13, pred[1024,1024]{0,1:T(8,128)(4,1)S(1)} %get-tuple-element.243, bf16[2,1,1024,128]{2,3,1,0:T(8,128)(2,1)} %get-tuple-element.289, s32[]{:T(128)S(6)} %select_n.115), kind=kOutput, calls=%fused_computation.17.clone.1 | convolution fusion | flops 1090519040 | bytes 20201476 | tf_op jit(solution)/shard_map/while/body/eval_jaxpr/gmn,nd->mgd/dot_general | solution.py:93
  291.1 5.2 %fusion.62 = bf16[1024,4,128]{0,2,1:T(8,128)(2,1)S(1)} fusion(f32[128,4,1024]{2,0,1:T(8,128)} %fusion.60, f32[1024,1024,4]{1,0,2:T(8,128)S(1)} %get-tuple-element.248, f32[4,1024]{1,0:T(4,128)S(1)} %max.13, pred[1024,1024]{0,1:T(8,128)(4,1)S(1)} %get-tuple-element.245, f32[1024,4]{0,1:T(4,128)S(1)} %add_bitcast_fusion.2, ...), kind=kOutput, calls=%fused_computation.25.clone.1 | convolution fusion | flops 1092091904 | bytes 21266436 | tf_op jit(solution)/shard_map/while/body/eval_jaxpr/gmn,nd->mgd/dot_general | solution.py:87
  296.4 0.5 copy.81
  296.9 1.0 constant_dynamic-update-slice_fusion.2
  298.0 31.5 %all_to_all.64 = bf16[8,256,512]{2,1,0:T(8,128)(2,1)S(1)} all-to-all(bf16[8,256,512]{2,1,0:T(8,128)(2,1)} %bitcast.168), channel_id=1, replica_groups=mesh['blk'=16,'uly'=8] {'uly'}, dimensions={0} | all-to-all | bytes 4194304 | tf_op jit(solution)/shard_map/all_to_all | solution.py:105
  329.5 2.4 copy.53
  331.9 4.1 %copy.54 = bf16[256,4096]{1,0:T(8,128)(2,1)} copy(bf16[256,4096]{0,1:T(8,128)(2,1)} %bitcast.165) | data formatting | bytes 4194304 | tf_op jit(solution)/shard_map/all_to_all | solution.py:105
  (24 shorter events, 0.1 us)
Async XLA Ops:
  6.5 18.8 %copy-start = (bf16[256,1024]{1,0:T(8,128)(2,1)S(1)}, bf16[256,1024]{1,0:T(8,128)(2,1)}, u32[]{:S(2)}) copy-start(bf16[256,1024]{1,0:T(8,128)(2,1)} %param.8) | copy-start | bytes 1572868
  6.5 30.7 %copy-start.2 = (bf16[256,4096]{1,0:T(8,128)(2,1)S(1)}, bf16[256,4096]{1,0:T(8,128)(2,1)}, u32[]{:S(2)}) copy-start(bf16[256,4096]{1,0:T(8,128)(2,1)} %param.7) | copy-start | bytes 6291460
  6.5 98.9 %all-gather.5.cloned.1.call-start = ((), (), s32[]{:S(2)}) async-start(), calls=%async_computation.5 | async-start | bytes 8912896 | tf_op jit(solution)/shard_map/all_gather | solution.py:50
  25.3 154.0 %all-gather.3.cloned.1.call-start = ((), (), s32[]{:S(2)}) async-start(), calls=%async_computation.4 | async-start | bytes 8912896 | tf_op jit(solution)/shard_map/all_gather | solution.py:49
  37.2 10.6 %copy-start.4 = (s32[4]{0:T(128)S(1)}, s32[4]{0:T(128)}, u32[]{:S(2)}) copy-start(s32[4]{0:T(128)} %param.10) | copy-start | bytes 52
  43.1 36.0 %all-to-all-start.2 = ((bf16[8,256,512]{2,1,0:T(8,128)(2,1)}), bf16[8,256,512]{2,1,0:T(8,128)(2,1)S(1)}, u32[]{:S(2)}, u32[]{:S(2)}) async-start(bf16[8,256,512]{2,1,0:T(8,128)(2,1)} %bitcast_dynamic-update-slice_fusion), calls=%async_computation.2 | async-start | bytes 4194304 | tf_op jit(solution)/shard_map/all_to_all | solution.py:23
  179.3 23.9 %copy-start.3 = (bf16[8,256,128]{2,1,0:T(8,128)(2,1)S(1)}, bf16[8,256,128]{2,1,0:T(8,128)(2,1)}, u32[]{:S(2)}) copy-start(bf16[8,256,128]{2,1,0:T(8,128)(2,1)} %copy.42) | copy-start | bytes 1572868
  329.5 6.4 %copy-start.1 = (bf16[256,1024]{1,0:T(8,128)(2,1)S(1)}, bf16[256,1024]{1,0:T(8,128)(2,1)}, u32[]{:S(2)}) copy-start(bf16[256,1024]{1,0:T(8,128)(2,1)} %param.8) | copy-start | bytes 1572868
Sparse Core Ops, SparseCore 0:
  25.4 79.9 all-gather.4
  107.9 71.3 all-gather.2
